TPU v7x, 256 devices: a whole 4x4x8 slice. The times are simulated.
256 devices in a mesh: panel: 16 (over y_hi, z), dir: 8 (over x, core), freq: 2 (over y_lo).
Axes of the slice: x: 4, y: 4 (y_hi: 2, y_lo: 2; y = y_hi * 2 + y_lo), z: 8, core: 2. Of those that a mesh axis runs over, the one named last changes fastest.
Arguments:
- sources: bfloat16 [4, 2, 64, 65536], P('freq', None, None, 'panel'), may hold values from -0.046875 to 0.046875
- panel_geom: float32 [4, 65536], P(None, 'panel'), may hold values from -150 to 150, as said below
- drift_cot: float32 [4, 64], P('freq'), may hold values from -4 to 4
- freq_index: int32 [4], P('freq'), may hold values from 0 to 511
- heading_dir: int32 [64], replicated, may hold values from 0 to 4095
Outputs:
- source_grad: float32 [4, 2, 64, 65536], P('freq', None, None, ('panel', 'dir'))
- geom_grad: float32 [4, 65536], P(None, ('panel', 'dir'))
Inputs may be any that keep to these rules, and one draw needn't show every extreme that they name: `panel_geom`: rows are panel centre x, y, z in metres, z at or below the water line, and panel area from 0.5 to 2.
All inputs are finite; a program needn't handle non-finite values.
Results may differ from a plain program's by a relative error of at most 0.00042.
Values may be sent and summed in bfloat16 or wider, within the bound.
A program may use at most 64 MiB of HBM per device.

v0:
```python
import math

import jax
import jax.numpy as jnp
from jax import lax
from jax.sharding import PartitionSpec as P

ND = 4096
FREQS = 512


gravity = 9.81
omega_low = 0.6
omega_span = 0.8
drift_gain = 5.0
cross_gain = 0.5
shape_scale = 100.0


def wave_numbers(freq_index):
    omega = omega_low + omega_span * freq_index.astype(jnp.float32) / FREQS
    return omega * omega / gravity


def direction_angles(dir_ids):
    return dir_ids.astype(jnp.float32) * (2.0 * math.pi / ND)


def phase_terms(geometry, wave, angles):
    amplitude = geometry[3] * jnp.exp(wave * geometry[2])
    phase = wave * (
        geometry[0][:, None] * jnp.cos(angles)[None, :]
        + geometry[1][:, None] * jnp.sin(angles)[None, :]
    )
    return (amplitude[:, None] * jnp.cos(phase), -amplitude[:, None] * jnp.sin(phase))


def kochin_block(sig, geometry, wave, dir_ids):
    heads = sig.shape[1]
    real, imag = phase_terms(geometry, wave, direction_angles(dir_ids))
    width = real.shape[1]
    phases = jnp.concatenate([real, imag], 1).astype(jnp.bfloat16)
    prod = jnp.dot(sig.reshape(2 * heads, sig.shape[2]), phases, preferred_element_type=jnp.float32)
    kreal = prod[:heads, :width] - prod[heads:, width:]
    kimag = prod[:heads, width:] + prod[heads:, :width]
    return jnp.stack([kreal, kimag])


def cotangent(kochin, wave, dir_ids, weight, heading_dir):
    angles = direction_angles(dir_ids)
    slope = -drift_gain * wave / math.sqrt(ND)
    beta = direction_angles(heading_dir)
    hit = (dir_ids[None, :] == heading_dir[:, None]).astype(jnp.float32)
    along = 2.0 * slope * jnp.cos(angles)[None, :]
    real_part = weight[:, None] * (along * kochin[0] - cross_gain * jnp.cos(beta)[:, None] * hit)
    imag_part = weight[:, None] * (along * kochin[1])
    return jnp.stack([real_part, imag_part]).astype(jnp.bfloat16)


def backward_block(sig, geometry, wave, dir_ids, cot):
    heads = sig.shape[1]
    angles = direction_angles(dir_ids)
    real, imag = phase_terms(geometry, wave, angles)
    width = real.shape[1]
    phases = jnp.concatenate([real, imag], 1).astype(jnp.bfloat16)
    mixed = jnp.concatenate(
        [jnp.concatenate([cot[0], cot[1]], 1), jnp.concatenate([cot[1], -cot[0]], 1)], 0
    )
    flat = sig.reshape(2 * heads, sig.shape[2])
    dsig = jnp.dot(mixed, phases.T, preferred_element_type=jnp.float32)
    dphase = jnp.dot(flat.T, mixed, preferred_element_type=jnp.float32)
    d_real = dphase[:, :width]
    d_imag = dphase[:, width:]
    twist = d_real * imag - d_imag * real
    swell = d_real * real + d_imag * imag
    shape = jnp.stack(
        [
            wave * jnp.sum(twist * jnp.cos(angles)[None, :], 1),
            wave * jnp.sum(twist * jnp.sin(angles)[None, :], 1),
            wave * jnp.sum(swell, 1),
            jnp.sum(swell, 1) / geometry[3],
        ]
    )
    return (dsig, shape)


def body(sources, panel_geom, drift_cot, freq_index, heading_dir):
    local_freqs = sources.shape[0]
    heads = sources.shape[2]
    panels = sources.shape[3]
    dir_count = ND // lax.axis_size("dir")
    dir_ids = lax.axis_index("dir") * dir_count + jnp.arange(dir_count, dtype=jnp.int32)
    waves = wave_numbers(freq_index)
    block = min(panels, 512)
    steps = panels // block
    kochin_parts = []
    for freq in range(local_freqs):

        def add_block(step, total):
            start = step * block
            sig = lax.dynamic_slice_in_dim(sources[freq], start, block, 2)
            geometry = lax.dynamic_slice_in_dim(panel_geom, start, block, 1)
            return total + kochin_block(sig, geometry, waves[freq], dir_ids)

        kochin_parts.append(
            lax.fori_loop(0, steps, add_block, jnp.zeros((2, heads, dir_count), jnp.float32))
        )
    partial_kochin = jnp.stack(kochin_parts)
    kochin = lax.psum(partial_kochin, "panel")
    cot = jnp.stack(
        [
            cotangent(kochin[freq], waves[freq], dir_ids, drift_cot[freq], heading_dir)
            for freq in range(local_freqs)
        ]
    )
    grads = []
    shape_total = jnp.zeros((4, panels), jnp.float32)
    for freq in range(local_freqs):

        def back_block(step, carry):
            grads_acc, shape_acc = carry
            start = step * block
            sig = lax.dynamic_slice_in_dim(sources[freq], start, block, 2)
            geometry = lax.dynamic_slice_in_dim(panel_geom, start, block, 1)
            dsig, shape = backward_block(sig, geometry, waves[freq], dir_ids, cot[freq])
            grads_acc = lax.dynamic_update_slice_in_dim(grads_acc, dsig, start, 1)
            old_shape = lax.dynamic_slice_in_dim(shape_acc, start, block, 1)
            shape_acc = lax.dynamic_update_slice_in_dim(shape_acc, old_shape + shape, start, 1)
            return (grads_acc, shape_acc)

        grads_freq, shape_total = lax.fori_loop(
            0, steps, back_block, (jnp.zeros((2 * heads, panels), jnp.float32), shape_total)
        )
        grads.append(grads_freq)
    grads_all = jnp.stack(grads).reshape(local_freqs, 2, heads, panels)
    source_part, shape_part = (
        lax.psum_scatter(grads_all, "dir", scatter_dimension=3, tiled=True),
        lax.psum_scatter(shape_total, "dir", scatter_dimension=1, tiled=True),
    )
    shape_all = lax.psum(shape_part, "freq")
    return (source_part, shape_scale * shape_all)


def solution(mesh):
    return jax.shard_map(
        body,
        mesh=mesh,
        in_specs=(
            P("freq", None, None, "panel"),
            P(None, "panel"),
            P("freq", None),
            P("freq"),
            P(),
        ),
        out_specs=(P("freq", None, None, ("panel", "dir")), P(None, ("panel", "dir"))),
        check_vma=False,
    )
```

profile of v0, /device:TPU:1, one launch (start us, length us, event | category | flops | bytes accessed | tf_op | source)
XLA Modules:
  0.0 534.6 jit_solution(602441275165219904)
XLA Ops:
  7.9 70.9 %while.75 = (s32[]{:T(128)}, f32[2,64,512]{2,1,0:T(8,128)S(1)}, bf16[2,2,64,4096]{3,2,1,0:T(8,128)(2,1)}, f32[4,4096]{1,0:T(4,128)}, f32[2]{0:T(128)S(1)}, /*ind...) while((s32[]{:T(128)}, f32[2,64,512]{2,1,0:T(8,128)S(1)}, ...), condition=%wide.region_3.0_spmd.clone, body=%wide.region_2.0_spmd.clone.sunk | while | flops 138677248 | bytes 6719753 | solution.py:106
  8.6 1.5 constant_dynamic-slice_fusion.23
  10.1 4.9 multiply_convert_fusion.7
  15.0 1.3 slice.600
  17.4 1.5 constant_dynamic-slice_fusion.23
  18.9 4.9 multiply_convert_fusion.7
  23.8 1.3 slice.600
  26.3 1.5 constant_dynamic-slice_fusion.23
  27.8 4.9 multiply_convert_fusion.7
  32.7 1.3 slice.600
  35.2 1.5 constant_dynamic-slice_fusion.23
  36.7 4.9 multiply_convert_fusion.7
  41.6 1.3 slice.600
  44.0 1.5 constant_dynamic-slice_fusion.23
  45.5 4.9 multiply_convert_fusion.7
  50.4 1.3 slice.600
  52.9 1.5 constant_dynamic-slice_fusion.23
  54.4 4.9 multiply_convert_fusion.7
  59.3 1.3 slice.600
  61.8 1.5 constant_dynamic-slice_fusion.23
  63.3 4.9 multiply_convert_fusion.7
  68.2 1.3 slice.600
  70.6 1.5 constant_dynamic-slice_fusion.23
  72.1 4.9 multiply_convert_fusion.7
  77.0 1.3 slice.600
  78.9 58.0 %while.74 = (s32[]{:T(128)}, f32[2,64,512]{2,1,0:T(8,128)S(1)}, bf16[2,2,64,4096]{3,2,1,0:T(8,128)(2,1)}, f32[4,4096]{1,0:T(4,128)}, f32[2]{0:T(128)S(1)}, /*ind...) while((s32[]{:T(128)}, f32[2,64,512]{2,1,0:T(8,128)S(1)}, ...), condition=%wide.region_1.0_spmd.clone, body=%wide.region_0.0_spmd.clone.sunk | while | flops 138677248 | bytes 6719745 | solution.py:106
  79.9 4.4 multiply_convert_fusion.6
  84.3 1.3 slice.597
  87.2 4.4 multiply_convert_fusion.6
  91.6 1.3 slice.597
  94.4 4.4 multiply_convert_fusion.6
  98.8 1.3 slice.597
  101.7 4.4 multiply_convert_fusion.6
  108.9 4.4 multiply_convert_fusion.6
  113.3 1.3 slice.597
  116.2 4.4 multiply_convert_fusion.6
  123.4 4.4 multiply_convert_fusion.6
  130.7 4.4 multiply_convert_fusion.6
  139.7 148.7 %all-reduce.2.cloned.1.call-done = f32[2,2,64,512]{3,2,1,0:T(8,128)} async-done(((f32[2,2,64,512]{3,2,1,0:T(8,128)}), f32[2,2,64,512]{3,2,1,0:T(8,128)}) %all-reduce.2.cloned.1.call-update) | async-done | bytes 524304 | tf_op jit(solution)/shard_map/psum | solution.py:109
  290.6 1.6 broadcast.578.clone2
  292.2 59.4 %while.72 = (s32[]{:T(128)}, f32[128,4096]{1,0:T(8,128)}, f32[4,4096]{1,0:T(4,128)S(1)}, f32[4,4096]{1,0:T(4,128)S(1)}, f32[2]{0:T(128)S(1)}, /*index=5*/bf16[12...) while((s32[]{:T(128)}, f32[128,4096]{1,0:T(8,128)}, ...), condition=%wide.region_9.10_spmd.clone, body=%wide.region_5.9_spmd.clone.sunk | while | flops 275526656 | bytes 10699039 | solution.py:131
  293.0 5.1 multiply_reduce_fusion.6
  300.4 5.1 multiply_reduce_fusion.6
  307.8 5.1 multiply_reduce_fusion.6
  315.2 5.1 multiply_reduce_fusion.6
  322.7 5.1 multiply_reduce_fusion.6
  330.1 5.1 multiply_reduce_fusion.6
  337.5 5.1 multiply_reduce_fusion.6
  344.9 5.1 multiply_reduce_fusion.6
  351.6 1.6 broadcast.578.clone
  353.1 88.5 %while.73 = (s32[]{:T(128)}, f32[128,4096]{1,0:T(8,128)}, f32[4,4096]{1,0:T(4,128)S(1)}, f32[4,4096]{1,0:T(4,128)S(1)}, f32[2]{0:T(128)S(1)}, /*index=5*/bf16[12...) while((s32[]{:T(128)}, f32[128,4096]{1,0:T(8,128)}, ...), condition=%wide.region_14.15_spmd.clone, body=%wide.region_10.14_spmd.clone.sunk | while | flops 275526656 | bytes 10699047 | solution.py:131
  355.1 5.7 %multiply_reduce_fusion.7 = (f32[512]{0:T(512)S(1)}, f32[512]{0:T(512)S(1)}, f32[512]{0:T(512)S(1)}, bf16[512,512]{1,0:T(8,128)(2,1)S(1)}, bf16[512,512]{1,0:T(8,128)(2,1)S(1)}) fusion(f32[512]{0:T(512)S(1)} %bitcast.240, f32[512]{0:T(512)S(1)} %bitcast.246, f32[512]{0:T(512)S(1)} %neg.91, f32[512,1024]{1,0:T(8,128)S(1)} %fusion.121, ...), kind=kLoop, calls=%fused_computation.39.clone.1 | loop fusion | flops 4979200 | bytes 3164164 | tf_op jit(solution)/shard_map/while/body/eval_jaxpr/reduce_sum | solution.py:78
  366.2 5.7 %multiply_reduce_fusion.7 = (f32[512]{0:T(512)S(1)}, f32[512]{0:T(512)S(1)}, f32[512]{0:T(512)S(1)}, bf16[512,512]{1,0:T(8,128)(2,1)S(1)}, bf16[512,512]{1,0:T(8,128)(2,1)S(1)}) fusion(f32[512]{0:T(512)S(1)} %bitcast.240, f32[512]{0:T(512)S(1)} %bitcast.246, f32[512]{0:T(512)S(1)} %neg.91, f32[512,1024]{1,0:T(8,128)S(1)} %fusion.121, ...), kind=kLoop, calls=%fused_computation.39.clone.1 | loop fusion | flops 4979200 | bytes 3164164 | tf_op jit(solution)/shard_map/while/body/eval_jaxpr/reduce_sum | solution.py:78
  377.2 5.7 %multiply_reduce_fusion.7 = (f32[512]{0:T(512)S(1)}, f32[512]{0:T(512)S(1)}, f32[512]{0:T(512)S(1)}, bf16[512,512]{1,0:T(8,128)(2,1)S(1)}, bf16[512,512]{1,0:T(8,128)(2,1)S(1)}) fusion(f32[512]{0:T(512)S(1)} %bitcast.240, f32[512]{0:T(512)S(1)} %bitcast.246, f32[512]{0:T(512)S(1)} %neg.91, f32[512,1024]{1,0:T(8,128)S(1)} %fusion.121, ...), kind=kLoop, calls=%fused_computation.39.clone.1 | loop fusion | flops 4979200 | bytes 3164164 | tf_op jit(solution)/shard_map/while/body/eval_jaxpr/reduce_sum | solution.py:78
  388.3 5.7 %multiply_reduce_fusion.7 = (f32[512]{0:T(512)S(1)}, f32[512]{0:T(512)S(1)}, f32[512]{0:T(512)S(1)}, bf16[512,512]{1,0:T(8,128)(2,1)S(1)}, bf16[512,512]{1,0:T(8,128)(2,1)S(1)}) fusion(f32[512]{0:T(512)S(1)} %bitcast.240, f32[512]{0:T(512)S(1)} %bitcast.246, f32[512]{0:T(512)S(1)} %neg.91, f32[512,1024]{1,0:T(8,128)S(1)} %fusion.121, ...), kind=kLoop, calls=%fused_computation.39.clone.1 | loop fusion | flops 4979200 | bytes 3164164 | tf_op jit(solution)/shard_map/while/body/eval_jaxpr/reduce_sum | solution.py:78
  399.4 5.7 %multiply_reduce_fusion.7 = (f32[512]{0:T(512)S(1)}, f32[512]{0:T(512)S(1)}, f32[512]{0:T(512)S(1)}, bf16[512,512]{1,0:T(8,128)(2,1)S(1)}, bf16[512,512]{1,0:T(8,128)(2,1)S(1)}) fusion(f32[512]{0:T(512)S(1)} %bitcast.240, f32[512]{0:T(512)S(1)} %bitcast.246, f32[512]{0:T(512)S(1)} %neg.91, f32[512,1024]{1,0:T(8,128)S(1)} %fusion.121, ...), kind=kLoop, calls=%fused_computation.39.clone.1 | loop fusion | flops 4979200 | bytes 3164164 | tf_op jit(solution)/shard_map/while/body/eval_jaxpr/reduce_sum | solution.py:78
  410.4 5.7 %multiply_reduce_fusion.7 = (f32[512]{0:T(512)S(1)}, f32[512]{0:T(512)S(1)}, f32[512]{0:T(512)S(1)}, bf16[512,512]{1,0:T(8,128)(2,1)S(1)}, bf16[512,512]{1,0:T(8,128)(2,1)S(1)}) fusion(f32[512]{0:T(512)S(1)} %bitcast.240, f32[512]{0:T(512)S(1)} %bitcast.246, f32[512]{0:T(512)S(1)} %neg.91, f32[512,1024]{1,0:T(8,128)S(1)} %fusion.121, ...), kind=kLoop, calls=%fused_computation.39.clone.1 | loop fusion | flops 4979200 | bytes 3164164 | tf_op jit(solution)/shard_map/while/body/eval_jaxpr/reduce_sum | solution.py:78
  421.5 5.7 %multiply_reduce_fusion.7 = (f32[512]{0:T(512)S(1)}, f32[512]{0:T(512)S(1)}, f32[512]{0:T(512)S(1)}, bf16[512,512]{1,0:T(8,128)(2,1)S(1)}, bf16[512,512]{1,0:T(8,128)(2,1)S(1)}) fusion(f32[512]{0:T(512)S(1)} %bitcast.240, f32[512]{0:T(512)S(1)} %bitcast.246, f32[512]{0:T(512)S(1)} %neg.91, f32[512,1024]{1,0:T(8,128)S(1)} %fusion.121, ...), kind=kLoop, calls=%fused_computation.39.clone.1 | loop fusion | flops 4979200 | bytes 3164164 | tf_op jit(solution)/shard_map/while/body/eval_jaxpr/reduce_sum | solution.py:78
  432.5 5.7 %multiply_reduce_fusion.7 = (f32[512]{0:T(512)S(1)}, f32[512]{0:T(512)S(1)}, f32[512]{0:T(512)S(1)}, bf16[512,512]{1,0:T(8,128)(2,1)S(1)}, bf16[512,512]{1,0:T(8,128)(2,1)S(1)}) fusion(f32[512]{0:T(512)S(1)} %bitcast.240, f32[512]{0:T(512)S(1)} %bitcast.246, f32[512]{0:T(512)S(1)} %neg.91, f32[512,1024]{1,0:T(8,128)S(1)} %fusion.121, ...), kind=kLoop, calls=%fused_computation.39.clone.1 | loop fusion | flops 4979200 | bytes 3164164 | tf_op jit(solution)/shard_map/while/body/eval_jaxpr/reduce_sum | solution.py:78
  441.6 2.0 copy.11
  443.7 3.9 pad_maximum_fusion
  447.6 38.2 %reduce-scatter.7.cloned.1.call-done = f32[512,4]{1,0:T(8,128)} async-done(((f32[4096,4]{1,0:T(8,128)}), f32[512,4]{1,0:T(8,128)}) %reduce-scatter.7.cloned.1.call-update) | async-done | bytes 8208
  486.9 3.8 psum.15
  491.3 36.8 %reduce-scatter.5.cloned.1.call-done = f32[2,2,64,512]{3,2,1,0:T(8,128)} async-done(((f32[2,2,64,4096]{3,2,1,0:T(8,128)}), f32[2,2,64,512]{3,2,1,0:T(8,128)}) %reduce-scatter.5.cloned.1.call-update) | async-done | bytes 524304 | tf_op jit(solution)/shard_map/reduce_scatter | solution.py:137
  (364 shorter events, 93.3 us)
Async XLA Ops:
  7.2 281.2 %all-reduce.2.cloned.1.call-start = ((), (), s32[]{:S(2)}) async-start(), calls=%async_computation.2 | async-start | bytes 1048576 | tf_op jit(solution)/shard_map/psum | solution.py:109
  78.8 60.8 %copy-start.4 = (s32[64]{0:T(128)S(1)}, s32[64]{0:T(128)}, u32[]{:S(2)}) copy-start(s32[64]{0:T(128)} %param.17) | copy-start | bytes 772
  78.8 60.9 %copy-start.3 = (f32[2,64]{1,0:T(2,128)S(1)}, f32[2,64]{1,0:T(2,128)}, u32[]{:S(2)}) copy-start(f32[2,64]{1,0:T(2,128)} %param.15) | copy-start | bytes 1540
  137.7 154.5 %copy-start = (bf16[2,2,64,4096]{3,2,1,0:T(8,128)(2,1)S(1)}, bf16[2,2,64,4096]{3,2,1,0:T(8,128)(2,1)}, u32[]{:S(2)}) copy-start(bf16[2,2,64,4096]{3,2,1,0:T(8,128)(2,1)} %get-tuple-element.1416) | copy-start | bytes 6291460
  137.7 154.5 %copy-start.2 = (f32[4,4096]{1,0:T(4,128)S(1)}, f32[4,4096]{1,0:T(4,128)}, u32[]{:S(2)}) copy-start(f32[4,4096]{1,0:T(4,128)} %get-tuple-element.1429) | copy-start | bytes 196612
  137.7 348.1 %reduce-scatter.7.cloned.1.call-start = ((), (), s32[]{:S(2)}) async-start(), calls=%async_computation.4 | async-start | bytes 2359296
  441.6 2.1 copy-start.1
  443.6 84.5 %reduce-scatter.5.cloned.1.call-start = ((), (), s32[]{:S(2)}) async-start(), calls=%async_computation.3 | async-start | bytes 4718592 | tf_op jit(solution)/shard_map/reduce_scatter | solution.py:137
Sparse Core Ops, SparseCore 0:
  137.8 150.5 all-reduce.1
  443.7 42.0 reduce-scatter.6
  488.9 39.1 reduce-scatter.4
where the time goes:
time: 539 us; the launch traced here: 535 us
  waiting for transfers between devices  224 us (42%)
  other arithmetic  218 us (40%)
  local copies, waits for them, and re-layouts  52.7 us (10%)
  matrix products  19 us (4%)
  between operations  15.1 us (3%)
    psum x1, waiting for transfers between devices, body(): kochin = lax.psum(partial_kochin, 'panel')  149 us
    reduce_sum x16, other arithmetic, backward_block(): jnp.sum(twist * jnp.cos(angles)[None, :], 1)  85.8 us
    another operation x16, other arithmetic  74.2 us
    unnamed x4, waiting for transfers between devices  38.3 us
    reduce_scatter x1, waiting for transfers between devices, body(): lax.psum_scatter(grads_all, 'dir', scatter_dimension=3, tiled=True)  36.8 us
    slice x32, other arithmetic, phase_terms(): geometry[0][:, None] * jnp.cos(angles)[None, :]  26.9 us
    slice x16, local copies, waits for them, and re-layouts, add_block(): sig = lax.dynamic_slice_in_dim(sources[freq], start, block, 2)  20.7 us
    dynamic_update_slice x32, local copies, waits for them, and re-layouts, back_block(): grads_acc = lax.dynamic_update_slice_in_dim(grads_acc, dsig, start, 1)  14.1 us
  transfers between devices with their start and end apart: 3, of which 3 were waited for; matrix products, arithmetic and copies ran while one was open for 1% of the time, Pallas kernels for 0%

commit v1 on v0

v1 whole, which is shorter than its diff:
```python
import functools
import math

import jax
import jax.numpy as jnp
import numpy as np
from jax import lax
from jax.experimental import pallas as pl
from jax.experimental.pallas import tpu as pltpu
from jax.sharding import PartitionSpec as P

ND = 4096
FREQS = 512
HALF = ND // 2

gravity = 9.81
omega_low = 0.6
omega_span = 0.8
drift_gain = 5.0
cross_gain = 0.5
shape_scale = 100.0

MESH = pl.DeviceIdType.MESH
F32 = jnp.float32
BF16 = jnp.bfloat16
ROUNDER = 1.5 * 2.0**23


def fit_even(values, degree):
    nodes = np.cos((2 * np.arange(400) + 1) * np.pi / 800)
    t = (nodes + 1) / 8
    cheb = np.polynomial.chebyshev.Chebyshev.fit(t, values(t), degree, domain=[0, 0.25])
    return [float(np.float32(c)) for c in cheb.convert(kind=np.polynomial.Polynomial).coef]


SIN_COEF = fit_even(lambda t: np.sinc(np.sqrt(t)) * np.pi, 4)
COS_COEF = fit_even(lambda t: np.cos(np.pi * np.sqrt(t)), 4)


def horner(coef, t):
    total = t * coef[-1] + coef[-2]
    for c in coef[-3::-1]:
        total = total * t + c
    return total


def half_angle(turns):
    r = turns - ((turns + ROUNDER) - ROUNDER)
    t = r * r
    return r * horner(SIN_COEF, t), horner(COS_COEF, t)


def kernel(
    sizes,
    src_hbm,
    geom_ref,
    cot_ref,
    fidx_ref,
    head_ref,
    table_ref,
    out_ref,
    geo_ref,
    src,
    vecs,
    ctab,
    stab,
    ef,
    eb,
    hpart,
    rsbuf,
    gall,
    lmat,
    lmat_t,
    dscr,
    ssend,
    sown,
    sbuf,
    xbuf,
    gsum,
    gbuf,
    src_sem,
    rs_send,
    rs_recv,
    ag_send,
    ag_recv,
    sib_send,
    sib_recv,
    x_send,
    x_recv,
    g_send,
    g_recv,
):
    npan, ndir, nfreq, nf, panels, block = sizes
    nx = ndir // 2
    dirs = HALF // ndir
    own = dirs // npan
    rows = 2 * own
    heads2 = src.shape[1]
    heads = heads2 // 2
    pi = lax.axis_index("panel")
    di = lax.axis_index("dir")
    fi = lax.axis_index("freq")
    x = di // 2
    core = di % 2

    copies = [pltpu.make_async_copy(src_hbm.at[f], src.at[f], src_sem.at[f]) for f in range(nf)]
    for c in copies:
        c.start()

    barrier = pltpu.get_barrier_semaphore()

    def greet_panel(o, carry):
        pl.semaphore_signal(barrier, inc=1, device_id={"panel": (pi + o) % npan}, device_id_type=MESH)
        return carry

    lax.fori_loop(1, npan, greet_panel, 0)
    for b in range(nfreq):

        def greet_dir(o, carry):
            pl.semaphore_signal(
                barrier,
                inc=1,
                device_id={"dir": (di + o) % ndir, "freq": (fi + b) % nfreq},
                device_id_type=MESH,
            )
            return carry

        lax.fori_loop(0 if b else 1, ndir, greet_dir, 0)

    for half in range(dirs // 128):
        row = di * (dirs // 128) + half
        at = pl.ds(half * 128, 128)
        ctab[at, :] = jnp.broadcast_to(table_ref[0, pl.ds(row, 1), :], (128, 128)).T
        stab[at, :] = jnp.broadcast_to(table_ref[1, pl.ds(row, 1), :], (128, 128)).T

    gsum[...] = jnp.zeros(gsum.shape, F32)
    for f in range(nf):
        omega = omega_low + omega_span * fidx_ref[f].astype(F32) / FREQS
        om = jnp.full((1, panels), omega, F32)
        k = om * om / gravity
        amp = geom_ref[3:4, :] * jnp.exp(k * geom_ref[2:3, :])
        vecs[f, 0:1, :] = k * geom_ref[0:1, :] * (0.5 / math.pi)
        vecs[f, 1:2, :] = k * geom_ref[1:2, :] * (0.5 / math.pi)
        vecs[f, 2:3, :] = amp
        vecs[f, 3:4, :] = -2.0 * amp
        vecs[f, 4:5, :] = k

    def forward(f):
        def step(b, carry):
            lanes = pl.ds(pl.multiple_of(b * block, block), block)

            def gen(g, inner):
                at = pl.ds(pl.multiple_of(g * own, own), own)
                ct = jnp.concatenate([ctab[at, :]] * (block // 128), axis=1)
                st = jnp.concatenate([stab[at, :]] * (block // 128), axis=1)
                turns = vecs[f, 0:1, lanes] * ct + vecs[f, 1:2, lanes] * st
                s, c = half_angle(turns)
                q = s * vecs[f, 3:4, lanes]
                re = vecs[f, 2:3, lanes] + q * s
                im = q * c
                base = pl.multiple_of(g * rows, rows)
                ef[f, pl.ds(base, own), lanes] = re
                ef[f, pl.ds(base + own, own), lanes] = im
                eb[f, pl.ds(base, own), lanes] = re.astype(BF16)
                eb[f, pl.ds(base + own, own), lanes] = im.astype(BF16)
                return inner

            lax.fori_loop(0, npan, gen, 0)
            hpart[f] += lax.dot_general(
                eb[f, :, lanes],
                src[f, :, lanes],
                (((1,), (1,)), ((), ())),
                preferred_element_type=F32,
            )
            return carry

        hpart[f] = jnp.zeros(hpart.shape[1:], F32)
        copies[f].wait()
        lax.fori_loop(0, panels // block, step, 0)

    def rs_copy(f, o):
        dest = (pi + o) % npan
        return pltpu.make_async_remote_copy(
            src_ref=hpart.at[f, pl.ds(pl.multiple_of(dest * rows, rows), rows)],
            dst_ref=rsbuf.at[f, o],
            send_sem=rs_send.at[f, o],
            recv_sem=rs_recv.at[f, o],
            device_id={"panel": dest},
            device_id_type=MESH,
        )

    def ag_copy(f, o):
        dest = (pi + o) % npan
        return pltpu.make_async_remote_copy(
            src_ref=gall.at[f, pi],
            dst_ref=gall.at[f, pi],
            send_sem=ag_send.at[f, o],
            recv_sem=ag_recv.at[f, o],
            device_id={"panel": dest},
            device_id_type=MESH,
        )

    def ag_arrival(f, o):
        origin = (pi - o + npan) % npan
        return pltpu.make_async_remote_copy(
            src_ref=gall.at[f, origin],
            dst_ref=gall.at[f, origin],
            send_sem=ag_send.at[f, o],
            recv_sem=ag_recv.at[f, o],
            device_id={"panel": origin},
            device_id_type=MESH,
        )

    def loop_over(lo, hi, fn):
        def step(o, carry):
            fn(o)
            return carry

        lax.fori_loop(lo, hi, step, 0)

    def cotangent(f):
        loop_over(1, npan, lambda o: rs_copy(f, o).wait_recv())
        total = hpart[f, pl.ds(pl.multiple_of(pi * rows, rows), rows), :]
        for o in range(1, npan):
            total = total + rsbuf[f, o]
        top = total[:own]
        low = pltpu.roll(total[own:], heads, 1)
        lane = lax.broadcasted_iota(jnp.int32, (own, heads2), 1)
        first = lane < heads
        sign = jnp.where(first, 1.0, -1.0)
        head = head_ref[...]
        sb, _ = half_angle(head.astype(F32) * (1.0 / ND))
        cosb = 1.0 - 2.0 * sb * sb
        ids = di * dirs + pi * own + lax.broadcasted_iota(jnp.int32, (own, heads2), 0)
        slope = vecs[f, 4:5, 0:heads2] * (-drift_gain) / math.sqrt(ND)
        along = 2.0 * slope * ctab[pl.ds(pl.multiple_of(pi * own, own), own), :] * sign
        weight = cot_ref[f : f + 1, :]
        pull = cross_gain * cosb
        hit = jnp.where((ids == head) & first, pull, 0.0)
        hit_far = jnp.where((ids + HALF == head) & first, pull, 0.0)
        near = weight * (along * (top - low) - hit)
        far = weight * (-along * (top + low) - hit_far)
        gall[f, pi] = jnp.concatenate([near, far], axis=1).astype(BF16)
        loop_over(1, npan, lambda o: ag_copy(f, o).start())

    def gather(f):
        loop_over(1, npan, lambda o: ag_arrival(f, o).wait_recv())

        def build(g, carry):
            near = gall[f, g, :, 0:heads2].astype(F32)
            far = gall[f, g, :, heads2:].astype(F32)
            top = jnp.concatenate([near, far], axis=1)
            low = jnp.concatenate([pltpu.roll(far, heads, 1), -pltpu.roll(near, heads, 1)], axis=1)
            both = jnp.concatenate([top, low], axis=0)
            base = pl.multiple_of(g * rows, rows)
            lmat[f, pl.ds(base, rows), :] = both.astype(BF16)
            return carry

        lax.fori_loop(0, npan, build, 0)
        for part in range(2 * dirs // 128):
            at = pl.ds(part * 128, 128)
            lmat_t[f, :, at] = lmat[f, at, :].astype(F32).T.astype(BF16)

    sub = 256

    def backward(f, xdest, side, dst):
        j = xdest * 2 + side

        def step(n, carry):
            lanes = pl.ds(pl.multiple_of(j * block + n * sub, sub), sub)
            w = src[f, :, lanes]
            both = jnp.dot(lmat_t[f], eb[f, :, lanes], preferred_element_type=F32)
            dst[:, pl.ds(pl.multiple_of(n * sub, sub), sub)] = both[:heads2] + both[heads2:]
            dscr[...] = jnp.dot(lmat[f], jnp.concatenate([w, w], axis=0), preferred_element_type=F32)

            def shape(g, acc):
                base = pl.multiple_of(g * rows, rows)
                at = pl.ds(pl.multiple_of(g * own, own), own)
                ct = jnp.concatenate([ctab[at, :]] * (sub // 128), axis=1)
                st = jnp.concatenate([stab[at, :]] * (sub // 128), axis=1)
                u = dscr[pl.ds(base, own), :]
                v = dscr[pl.ds(base + own, own), :]
                re = ef[f, pl.ds(base, own), lanes]
                im = ef[f, pl.ds(base + own, own), lanes]
                twist = u * im - v * re
                swell = u * re + v * im
                terms = (twist * ct, twist * st, swell)
                return tuple(
                    a + sum(t[8 * i : 8 * i + 8] for i in range(own // 8))
                    for a, t in zip(acc, terms)
                )

            zero = jnp.zeros((8, sub), F32)
            qc, qs, rs = lax.fori_loop(0, npan, shape, (zero, zero, zero))
            k = vecs[f, 4:5, lanes]
            qc = k * jnp.sum(qc, axis=0, keepdims=True)
            qs = k * jnp.sum(qs, axis=0, keepdims=True)
            rs = jnp.sum(rs, axis=0, keepdims=True)
            here = pl.ds(pl.multiple_of(n * sub, sub), sub)
            for r, value in enumerate((qc, qs, k * rs, rs)):
                gsum[j, r : r + 1, here] += value
            return carry

        lax.fori_loop(0, block // sub, step, 0)

    xp = (x + 1) % nx
    xm = (x + nx - 1) % nx
    x2 = (x + 2) % nx
    order = (x2, xp, xm, x)

    def sib_copy(f, n):
        return pltpu.make_async_remote_copy(
            src_ref=ssend.at[f, n],
            dst_ref=sbuf.at[f, n],
            send_sem=sib_send.at[f, n],
            recv_sem=sib_recv.at[f, n],
            device_id={"dir": x * 2 + (1 - core)},
            device_id_type=MESH,
        )

    upper, lower = pl.ds(0, heads), pl.ds(heads, heads)
    messages = (
        (0, upper, xp),
        (0, lower, xm),
        (1, lower, xp),
        (1, upper, xp),
        (2, upper, xm),
        (2, lower, xm),
    )

    def x_copy(f, m):
        n, part, to = messages[m]
        return pltpu.make_async_remote_copy(
            src_ref=sown.at[f, n, part],
            dst_ref=xbuf.at[f, m],
            send_sem=x_send.at[f, m],
            recv_sem=x_recv.at[f, m],
            device_id={"dir": to * 2 + core},
            device_id_type=MESH,
        )

    def to_sibling(f, n):
        backward(f, order[n], 1 - core, ssend.at[f, n])
        sib_copy(f, n).start()

    def keep(f, n):
        backward(f, order[n], core, sown.at[f, n])

    def join(f, n):
        sib_copy(f, n).wait_recv()
        sown[f, n] += sbuf[f, n]

    def reverse(f):
        to_sibling(f, 0)
        keep(f, 0)
        to_sibling(f, 1)
        join(f, 0)
        x_copy(f, 0).start()
        x_copy(f, 1).start()
        keep(f, 1)
        to_sibling(f, 2)
        join(f, 1)
        x_copy(f, 2).start()
        keep(f, 2)
        to_sibling(f, 3)
        join(f, 2)
        x_copy(f, 4).start()
        keep(f, 3)

    def relay(f):
        x_copy(f, 0).wait_recv()
        sown[f, 1, upper] += xbuf[f, 0]
        x_copy(f, 3).start()
        x_copy(f, 1).wait_recv()
        sown[f, 2, lower] += xbuf[f, 1]
        x_copy(f, 5).start()

    def finish(f):
        sib_copy(f, 3).wait_recv()
        for m in (2, 3, 4, 5):
            x_copy(f, m).wait_recv()
        total = sown[f, 3] + sbuf[f, 3]
        out_ref[f, upper] = total[:heads] + xbuf[f, 3] + xbuf[f, 4]
        out_ref[f, lower] = total[heads:] + xbuf[f, 2] + xbuf[f, 5]

    def g_copy(b, o):
        to = (di + o) % ndir
        return pltpu.make_async_remote_copy(
            src_ref=gsum.at[to],
            dst_ref=gbuf.at[b, o],
            send_sem=g_send.at[b, o],
            recv_sem=g_recv.at[b, o],
            device_id={"dir": to, "freq": (fi + b) % nfreq},
            device_id_type=MESH,
        )

    for f in range(nf):
        forward(f)
        if f == 0:
            pl.semaphore_wait(barrier, npan - 1 + nfreq * ndir - 1)
        loop_over(1, npan, lambda o: rs_copy(f, o).start())
    for f in range(nf):
        cotangent(f)
    gather(0)
    reverse(0)
    gather(1)
    relay(0)
    reverse(1)
    for b in range(nfreq):
        loop_over(0 if b else 1, ndir, lambda o: g_copy(b, o).start())
    relay(1)
    finish(0)
    for b in range(nfreq):
        loop_over(0 if b else 1, ndir, lambda o: g_copy(b, o).wait_recv())
    total = gsum[di]
    for b in range(nfreq):
        for o in range(0 if b else 1, ndir):
            total = total + gbuf[b, o]
    area = geom_ref[3:4, pl.ds(pl.multiple_of(di * block, block), block)]
    geo_ref[0:3, :] = shape_scale * total[0:3]
    geo_ref[3:4, :] = shape_scale * (total[3:4] / area)
    finish(1)

    for f in range(nf):
        loop_over(1, npan, lambda o: rs_copy(f, o).wait_send())
        loop_over(1, npan, lambda o: ag_copy(f, o).wait_send())
        for n in range(4):
            sib_copy(f, n).wait_send()
        for m in range(6):
            x_copy(f, m).wait_send()
    for b in range(nfreq):
        loop_over(0 if b else 1, ndir, lambda o: g_copy(b, o).wait_send())


def direction_table():
    angle = np.arange(HALF, dtype=np.float64) * (2.0 * np.pi / ND)
    return np.stack([np.cos(angle), np.sin(angle)]).astype(np.float32).reshape(2, HALF // 128, 128)


def solution(mesh):
    npan, ndir, nfreq = (mesh.shape[a] for a in ("panel", "dir", "freq"))

    def body(sources, panel_geom, drift_cot, freq_index, heading_dir):
        nf, parts, heads, panels = sources.shape
        block = panels // ndir
        dirs = HALF // ndir
        own = dirs // npan
        heads2 = 2 * heads
        sizes = (npan, ndir, nfreq, nf, panels, block)
        dma = pltpu.SemaphoreType.DMA
        vmem = pltpu.VMEM
        out, geo = pl.pallas_call(
            functools.partial(kernel, sizes),
            out_shape=(
                jax.ShapeDtypeStruct((nf, heads2, block), F32),
                jax.ShapeDtypeStruct((4, block), F32),
            ),
            in_specs=[
                pl.BlockSpec(memory_space=pl.ANY),
                pl.BlockSpec(memory_space=vmem),
                pl.BlockSpec(memory_space=vmem),
                pl.BlockSpec(memory_space=pltpu.SMEM),
                pl.BlockSpec(memory_space=vmem),
                pl.BlockSpec(memory_space=vmem),
            ],
            out_specs=(pl.BlockSpec(memory_space=vmem), pl.BlockSpec(memory_space=vmem)),
            scratch_shapes=[
                vmem((nf, heads2, panels), BF16),
                vmem((nf, 8, panels), F32),
                vmem((dirs, 128), F32),
                vmem((dirs, 128), F32),
                vmem((nf, 2 * dirs, panels), F32),
                vmem((nf, 2 * dirs, panels), BF16),
                vmem((nf, 2 * dirs, heads2), F32),
                vmem((nf, npan, 2 * own, heads2), F32),
                vmem((nf, npan, own, 2 * heads2), BF16),
                vmem((nf, 2 * dirs, 2 * heads2), BF16),
                vmem((nf, 2 * heads2, 2 * dirs), BF16),
                vmem((2 * dirs, 256), F32),
                vmem((nf, 4, heads2, block), F32),
                vmem((nf, 4, heads2, block), F32),
                vmem((nf, 4, heads2, block), F32),
                vmem((nf, 6, heads, block), F32),
                vmem((ndir, 8, block), F32),
                vmem((nfreq, ndir, 8, block), F32),
                dma((nf,)),
                dma((nf, npan)),
                dma((nf, npan)),
                dma((nf, npan)),
                dma((nf, npan)),
                dma((nf, 4)),
                dma((nf, 4)),
                dma((nf, 6)),
                dma((nf, 6)),
                dma((nfreq, ndir)),
                dma((nfreq, ndir)),
            ],
            compiler_params=pltpu.CompilerParams(
                collective_id=0, has_side_effects=True, vmem_limit_bytes=60 * 1024 * 1024
            ),
        )(
            sources.reshape(nf, heads2, panels),
            panel_geom,
            jnp.concatenate([drift_cot, drift_cot], axis=1),
            freq_index,
            jnp.concatenate([heading_dir, heading_dir]).reshape(1, heads2),
            jnp.asarray(direction_table()),
        )
        return out.reshape(nf, parts, heads, block), geo

    return jax.shard_map(
        body,
        mesh=mesh,
        in_specs=(
            P("freq", None, None, "panel"),
            P(None, "panel"),
            P("freq", None),
            P("freq"),
            P(),
        ),
        out_specs=(P("freq", None, None, ("panel", "dir")), P(None, ("panel", "dir"))),
        check_vma=False,
    )
```

time: 539 us -> 75.3 us (0.14)
  waiting for transfers between devices: 224 us -> 0 us
  other arithmetic: 218 us -> 2.7 us
  Pallas kernels: 0 us -> 68.5 us
  local copies, waits for them, and re-layouts: 52.7 us -> 3.16 us
  matrix products: 19 us -> 0 us
  between operations: 15.1 us -> 0.64 us
    psum x1 -> x0, waiting for transfers between devices: 149 us -> none  [body(): kochin = lax.psum(partial_kochin, 'panel')]
    reduce_sum x16 -> x0, other arithmetic: 85.8 us -> none  [backward_block(): jnp.sum(twist * jnp.cos(angles)[None, :], 1)]
    another operation x34 -> x0, other arithmetic: 79.5 us -> none
    pallas_call x0 -> x1, Pallas kernels: none -> 68.5 us  [body(): pl.pallas_call(functools.partial(kernel, sizes), out_shape=(jax.ShapeDtyp...]
    unnamed x4 -> x0, waiting for transfers between devices: 38.3 us -> none
    reduce_scatter x1 -> x0, waiting for transfers between devices: 36.8 us -> none  [body(): lax.psum_scatter(grads_all, 'dir', scatter_dimension=3, tiled=True)]
    slice x50 -> x0, local copies, waits for them, and re-layouts: 31.9 us -> none  [the longest x16 20.7 us: add_block(): sig = lax.dynamic_slice_in_dim(sources[freq], start, block, 2)]
    slice x32 -> x0, other arithmetic: 26.9 us -> none  [phase_terms(): geometry[0][:, None] * jnp.cos(angles)[None, :]]
  transfers between devices with their start and end apart: 3 -> 0, of which waited for: 3 -> 0; matrix products, arithmetic and copies ran while one was open for 1% -> 0% of each run, Pallas kernels for 0% -> 0%
where the time goes in v1:
time: 75.3 us; the launch traced here: 75 us
  Pallas kernels  68.5 us (91%)
  local copies, waits for them, and re-layouts  3.16 us (4%)
  other arithmetic  2.7 us (4%)
    pallas_call x1, Pallas kernels, body(): pl.pallas_call(functools.partial(kernel, sizes), out_shape=(jax.ShapeDtyp...  68.5 us
    unnamed x2, local copies, waits for them, and re-layouts  3.16 us

profile of v1, /device:TPU:1, one launch (start us, length us, event | category | flops | bytes accessed | tf_op | source)
XLA Modules:
  0.0 75.0 jit_solution(7138544871766875852)
XLA Ops:
  0.6 1.3 %add_bitcast_fusion.head_ref = s32[1,128]{1,0:T(1,128)} fusion(s32[64]{0:T(128)} %param.10), kind=kLoop, calls=%fused_computation.1 | loop fusion | flops 128 | bytes 768 | tf_op jit(solution)/shard_map/reshape | solution.py:506
  1.9 1.4 %pad_maximum_fusion.cot_ref = f32[2,128]{1,0:T(2,128)} fusion(f32[2,64]{1,0:T(2,128)} %param.8), kind=kLoop, calls=%fused_computation | loop fusion | flops 256 | bytes 1536 | tf_op jit(solution)/shard_map/concatenate | solution.py:504
  3.3 68.5 %shard_map.77 = (f32[2,128,512]{2,1,0:T(8,128)}, f32[4,512]{1,0:T(4,128)}) custom-call(bf16[2,128,4096]{2,1,0:T(8,128)(2,1)} %bitcast.4, f32[4,4096]{1,0:T(4,128)} %geom_ref.1, f32[2,128]{1,0:T(2,128)} %pad_maximum_fusion.cot_ref, s32[2]{0:T(128)} %fidx_ref.1, s32[1,128]{1,0:T(1,128)} %add_bitcast_fusion.head_ref, f32[2,16,128]{2,1,0:T(8,128)} %constant.2.clone.table_ref), custom_call_target="tpu_custom_call" | custom-call | tf_op jit(solution)/shard_map/pallas_call | solution.py:452
  71.8 1.9 %copy.10 = f32[2,2,64,512]{3,2,1,0:T(8,128)} copy(f32[2,2,64,512]{3,2,1,0:T(8,128)} %bitcast.5) | data formatting | bytes 1048576
  73.7 1.3 %copy.11 = f32[4,512]{1,0:T(4,128)} copy(f32[4,512]{1,0:T(4,128)} %get-tuple-element.9) | data formatting | bytes 16384

commit v2 on v1

--- a/solution.py
+++ b/solution.py
@@ -75,7 +75,10 @@
     ssend,
     sown,
     sbuf,
-    xbuf,
+    qsend,
+    qrecv,
+    msend,
+    mrecv,
     gsum,
     gbuf,
     src_sem,
@@ -144,13 +147,14 @@
         vecs[f, 2:3, :] = amp
         vecs[f, 3:4, :] = -2.0 * amp
         vecs[f, 4:5, :] = k
+        vecs[f, 5:6, :] = 1.0 / amp
 
     def forward(f):
         def step(b, carry):
             lanes = pl.ds(pl.multiple_of(b * block, block), block)
 
-            def gen(g, inner):
-                at = pl.ds(pl.multiple_of(g * own, own), own)
+            for g in range(npan):
+                at = pl.ds(g * own, own)
                 ct = jnp.concatenate([ctab[at, :]] * (block // 128), axis=1)
                 st = jnp.concatenate([stab[at, :]] * (block // 128), axis=1)
                 turns = vecs[f, 0:1, lanes] * ct + vecs[f, 1:2, lanes] * st
@@ -158,14 +162,11 @@
                 q = s * vecs[f, 3:4, lanes]
                 re = vecs[f, 2:3, lanes] + q * s
                 im = q * c
-                base = pl.multiple_of(g * rows, rows)
+                base = g * rows
                 ef[f, pl.ds(base, own), lanes] = re
                 ef[f, pl.ds(base + own, own), lanes] = im
                 eb[f, pl.ds(base, own), lanes] = re.astype(BF16)
                 eb[f, pl.ds(base + own, own), lanes] = im.astype(BF16)
-                return inner
-
-            lax.fori_loop(0, npan, gen, 0)
             hpart[f] += lax.dot_general(
                 eb[f, :, lanes],
                 src[f, :, lanes],
@@ -228,13 +229,13 @@
         lane = lax.broadcasted_iota(jnp.int32, (own, heads2), 1)
         first = lane < heads
         sign = jnp.where(first, 1.0, -1.0)
-        head = head_ref[...]
+        head = jnp.concatenate([head_ref[...]] * 2, axis=1)
         sb, _ = half_angle(head.astype(F32) * (1.0 / ND))
         cosb = 1.0 - 2.0 * sb * sb
         ids = di * dirs + pi * own + lax.broadcasted_iota(jnp.int32, (own, heads2), 0)
         slope = vecs[f, 4:5, 0:heads2] * (-drift_gain) / math.sqrt(ND)
         along = 2.0 * slope * ctab[pl.ds(pl.multiple_of(pi * own, own), own), :] * sign
-        weight = cot_ref[f : f + 1, :]
+        weight = jnp.concatenate([cot_ref[f : f + 1, :]] * 2, axis=1)
         pull = cross_gain * cosb
         hit = jnp.where((ids == head) & first, pull, 0.0)
         hit_far = jnp.where((ids + HALF == head) & first, pull, 0.0)
@@ -246,17 +247,13 @@
     def gather(f):
         loop_over(1, npan, lambda o: ag_arrival(f, o).wait_recv())
 
-        def build(g, carry):
+        for g in range(npan):
             near = gall[f, g, :, 0:heads2].astype(F32)
             far = gall[f, g, :, heads2:].astype(F32)
             top = jnp.concatenate([near, far], axis=1)
             low = jnp.concatenate([pltpu.roll(far, heads, 1), -pltpu.roll(near, heads, 1)], axis=1)
             both = jnp.concatenate([top, low], axis=0)
-            base = pl.multiple_of(g * rows, rows)
-            lmat[f, pl.ds(base, rows), :] = both.astype(BF16)
-            return carry
-
-        lax.fori_loop(0, npan, build, 0)
+            lmat[f, pl.ds(g * rows, rows), :] = both.astype(BF16)
         for part in range(2 * dirs // 128):
             at = pl.ds(part * 128, 128)
             lmat_t[f, :, at] = lmat[f, at, :].astype(F32).T.astype(BF16)
@@ -273,9 +270,11 @@
             dst[:, pl.ds(pl.multiple_of(n * sub, sub), sub)] = both[:heads2] + both[heads2:]
             dscr[...] = jnp.dot(lmat[f], jnp.concatenate([w, w], axis=0), preferred_element_type=F32)
 
-            def shape(g, acc):
-                base = pl.multiple_of(g * rows, rows)
-                at = pl.ds(pl.multiple_of(g * own, own), own)
+            zero = jnp.zeros((8, sub), F32)
+            acc = (zero, zero, zero)
+            for g in range(npan):
+                base = g * rows
+                at = pl.ds(g * own, own)
                 ct = jnp.concatenate([ctab[at, :]] * (sub // 128), axis=1)
                 st = jnp.concatenate([stab[at, :]] * (sub // 128), axis=1)
                 u = dscr[pl.ds(base, own), :]
@@ -285,13 +284,11 @@
                 twist = u * im - v * re
                 swell = u * re + v * im
                 terms = (twist * ct, twist * st, swell)
-                return tuple(
+                acc = tuple(
                     a + sum(t[8 * i : 8 * i + 8] for i in range(own // 8))
                     for a, t in zip(acc, terms)
                 )
-
-            zero = jnp.zeros((8, sub), F32)
-            qc, qs, rs = lax.fori_loop(0, npan, shape, (zero, zero, zero))
+            qc, qs, rs = acc
             k = vecs[f, 4:5, lanes]
             qc = k * jnp.sum(qc, axis=0, keepdims=True)
             qs = k * jnp.sum(qs, axis=0, keepdims=True)
@@ -328,16 +325,55 @@
         (2, lower, xm),
     )
 
-    def x_copy(f, m):
-        n, part, to = messages[m]
-        return pltpu.make_async_remote_copy(
-            src_ref=sown.at[f, n, part],
-            dst_ref=xbuf.at[f, m],
-            send_sem=x_send.at[f, m],
-            recv_sem=x_recv.at[f, m],
-            device_id={"dir": to * 2 + core},
-            device_id_type=MESH,
-        )
+    def x_copies(f, m):
+        to = messages[m][2]
+        return [
+            pltpu.make_async_remote_copy(
+                src_ref=out_at.at[f, m],
+                dst_ref=in_at.at[f, m],
+                send_sem=x_send.at[f, m, i],
+                recv_sem=x_recv.at[f, m, i],
+                device_id={"dir": to * 2 + core},
+                device_id_type=MESH,
+            )
+            for i, (out_at, in_at) in enumerate(((qsend, qrecv), (msend, mrecv)))
+        ]
+
+    def block_lanes(n):
+        return pl.ds(pl.multiple_of((order[n] * 2 + core) * block, block), block)
+
+    lane = lax.broadcasted_iota(jnp.int32, (8, 128), 1)
+
+    def x_start(f, m):
+        n, part, _ = messages[m]
+        value = sown[f, n, part] * vecs[f, 5:6, block_lanes(n)]
+        top = jnp.maximum(jnp.max(jnp.abs(value), axis=1, keepdims=True), 1e-30)
+        level = value * (32000.0 / top)
+        level = (level + ROUNDER) - ROUNDER
+        qsend[f, m] = level.astype(jnp.int32).astype(jnp.int16)
+        unit = jnp.broadcast_to(top * (1.0 / 32000.0), (heads, 128))
+        packed = unit[0:8]
+        for i in range(1, heads // 8):
+            packed = jnp.where(lane >= 16 * i, unit[8 * i : 8 * i + 8], packed)
+        msend[f, m] = packed
+        for c in x_copies(f, m):
+            c.start()
+
+    def x_read(f, m, n):
+        level = qrecv[f, m].astype(jnp.int32).astype(F32)
+        unit = mrecv[f, m]
+        unit = jnp.concatenate(
+            [
+                jnp.broadcast_to(unit[:, 16 * i : 16 * i + 1], (8, block))
+                for i in range(heads // 8)
+            ],
+            axis=0,
+        )
+        return level * unit * vecs[f, 2:3, block_lanes(n)]
+
+    def x_wait(f, m):
+        for c in x_copies(f, m):
+            c.wait_recv()
 
     def to_sibling(f, n):
         backward(f, order[n], 1 - core, ssend.at[f, n])
@@ -355,33 +391,33 @@
         keep(f, 0)
         to_sibling(f, 1)
         join(f, 0)
-        x_copy(f, 0).start()
-        x_copy(f, 1).start()
+        x_start(f, 0)
+        x_start(f, 1)
         keep(f, 1)
         to_sibling(f, 2)
         join(f, 1)
-        x_copy(f, 2).start()
+        x_start(f, 2)
         keep(f, 2)
         to_sibling(f, 3)
         join(f, 2)
-        x_copy(f, 4).start()
+        x_start(f, 4)
         keep(f, 3)
 
     def relay(f):
-        x_copy(f, 0).wait_recv()
-        sown[f, 1, upper] += xbuf[f, 0]
-        x_copy(f, 3).start()
-        x_copy(f, 1).wait_recv()
-        sown[f, 2, lower] += xbuf[f, 1]
-        x_copy(f, 5).start()
+        x_wait(f, 0)
+        sown[f, 1, upper] += x_read(f, 0, 1)
+        x_start(f, 3)
+        x_wait(f, 1)
+        sown[f, 2, lower] += x_read(f, 1, 2)
+        x_start(f, 5)
 
     def finish(f):
         sib_copy(f, 3).wait_recv()
-        for m in (2, 3, 4, 5):
-            x_copy(f, m).wait_recv()
+        for m in (2, 4, 3, 5):
+            x_wait(f, m)
         total = sown[f, 3] + sbuf[f, 3]
-        out_ref[f, upper] = total[:heads] + xbuf[f, 3] + xbuf[f, 4]
-        out_ref[f, lower] = total[heads:] + xbuf[f, 2] + xbuf[f, 5]
+        out_ref[f, upper] = total[:heads] + x_read(f, 3, 3) + x_read(f, 4, 3)
+        out_ref[f, lower] = total[heads:] + x_read(f, 2, 3) + x_read(f, 5, 3)
 
     def g_copy(b, o):
         to = (di + o) % ndir
@@ -427,7 +463,8 @@
         for n in range(4):
             sib_copy(f, n).wait_send()
         for m in range(6):
-            x_copy(f, m).wait_send()
+            for c in x_copies(f, m):
+                c.wait_send()
     for b in range(nfreq):
         loop_over(0 if b else 1, ndir, lambda o: g_copy(b, o).wait_send())
 
@@ -480,7 +517,10 @@
                 vmem((nf, 4, heads2, block), F32),
                 vmem((nf, 4, heads2, block), F32),
                 vmem((nf, 4, heads2, block), F32),
-                vmem((nf, 6, heads, block), F32),
+                vmem((nf, 6, heads, block), jnp.int16),
+                vmem((nf, 6, heads, block), jnp.int16),
+                vmem((nf, 6, 8, 128), F32),
+                vmem((nf, 6, 8, 128), F32),
                 vmem((ndir, 8, block), F32),
                 vmem((nfreq, ndir, 8, block), F32),
                 dma((nf,)),
@@ -490,8 +530,8 @@
                 dma((nf, npan)),
                 dma((nf, 4)),
                 dma((nf, 4)),
-                dma((nf, 6)),
-                dma((nf, 6)),
+                dma((nf, 6, 2)),
+                dma((nf, 6, 2)),
                 dma((nfreq, ndir)),
                 dma((nfreq, ndir)),
             ],
@@ -501,9 +541,9 @@
         )(
             sources.reshape(nf, heads2, panels),
             panel_geom,
-            jnp.concatenate([drift_cot, drift_cot], axis=1),
+            drift_cot,
             freq_index,
-            jnp.concatenate([heading_dir, heading_dir]).reshape(1, heads2),
+            heading_dir.reshape(1, heads),
             jnp.asarray(direction_table()),
         )
         return out.reshape(nf, parts, heads, block), geo

time: 75.3 us -> 60.3 us (0.80)
  Pallas kernels: 68.5 us -> 56.3 us
  other arithmetic: 2.7 us -> 0 us
    pallas_call x1, Pallas kernels: 68.5 us -> 56.3 us  [body(): pl.pallas_call(functools.partial(kernel, sizes), out_shape=(jax.ShapeDtyp...]
    concatenate x1 -> x0, other arithmetic: 1.39 us -> none  [body(): jnp.concatenate([drift_cot, drift_cot], axis=1)]
    reshape x1 -> x0, other arithmetic: 1.31 us -> none  [body(): jnp.concatenate([heading_dir, heading_dir]).reshape(1, heads2)]
where the time goes in v2:
time: 60.3 us; the launch traced here: 60.1 us
  Pallas kernels  56.3 us (93%)
  local copies, waits for them, and re-layouts  3.16 us (5%)
  between operations  0.64 us (1%)
    pallas_call x1, Pallas kernels, body(): pl.pallas_call(functools.partial(kernel, sizes), out_shape=(jax.ShapeDtyp...  56.3 us
    unnamed x2, local copies, waits for them, and re-layouts  3.16 us

profile of v2, /device:TPU:1, one launch (start us, length us, event | category | flops | bytes accessed | tf_op | source)
XLA Modules:
  0.0 60.1 jit_solution(12057893253199803488)
XLA Ops:
  0.6 56.3 %shard_map.77 = (f32[2,128,512]{2,1,0:T(8,128)}, f32[4,512]{1,0:T(4,128)}) custom-call(bf16[2,128,4096]{2,1,0:T(8,128)(2,1)} %bitcast.3, f32[4,4096]{1,0:T(4,128)} %geom_ref.1, f32[2,64]{1,0:T(2,128)} %cot_ref.1, s32[2]{0:T(128)} %fidx_ref.1, s32[1,64]{1,0:T(1,128)} %bitcast.5, f32[2,16,128]{2,1,0:T(8,128)} %constant.2.clone.table_ref), custom_call_target="tpu_custom_call" | custom-call | tf_op jit(solution)/shard_map/pallas_call | solution.py:489
  56.9 1.9 %copy.10 = f32[2,2,64,512]{3,2,1,0:T(8,128)} copy(f32[2,2,64,512]{3,2,1,0:T(8,128)} %bitcast.4) | data formatting | bytes 1048576
  58.8 1.3 %copy.11 = f32[4,512]{1,0:T(4,128)} copy(f32[4,512]{1,0:T(4,128)} %get-tuple-element.9) | data formatting | bytes 16384

commit v3 on v2

--- a/solution.py
+++ b/solution.py
@@ -33,7 +33,7 @@
     return [float(np.float32(c)) for c in cheb.convert(kind=np.polynomial.Polynomial).coef]
 
 
-SIN_COEF = fit_even(lambda t: np.sinc(np.sqrt(t)) * np.pi, 4)
+SIN_COEF = fit_even(lambda t: np.sinc(np.sqrt(t)) * np.pi, 3)
 COS_COEF = fit_even(lambda t: np.cos(np.pi * np.sqrt(t)), 4)
 
 
@@ -67,6 +67,7 @@
     ef,
     eb,
     hpart,
+    pairbuf,
     rsbuf,
     gall,
     lmat,
@@ -82,6 +83,8 @@
     gsum,
     gbuf,
     src_sem,
+    pair_send,
+    pair_recv,
     rs_send,
     rs_recv,
     ag_send,
@@ -137,7 +140,7 @@
         stab[at, :] = jnp.broadcast_to(table_ref[1, pl.ds(row, 1), :], (128, 128)).T
 
     gsum[...] = jnp.zeros(gsum.shape, F32)
-    for f in range(nf):
+    def prepare(f):
         omega = omega_low + omega_span * fidx_ref[f].astype(F32) / FREQS
         om = jnp.full((1, panels), omega, F32)
         k = om * om / gravity
@@ -149,11 +152,13 @@
         vecs[f, 4:5, :] = k
         vecs[f, 5:6, :] = 1.0 / amp
 
-    def forward(f):
+    def forward(f, lo, hi):
+        some = pl.ds(lo * rows, (hi - lo) * rows)
+
         def step(b, carry):
             lanes = pl.ds(pl.multiple_of(b * block, block), block)
 
-            for g in range(npan):
+            for g in range(lo, hi):
                 at = pl.ds(g * own, own)
                 ct = jnp.concatenate([ctab[at, :]] * (block // 128), axis=1)
                 st = jnp.concatenate([stab[at, :]] * (block // 128), axis=1)
@@ -167,20 +172,36 @@
                 ef[f, pl.ds(base + own, own), lanes] = im
                 eb[f, pl.ds(base, own), lanes] = re.astype(BF16)
                 eb[f, pl.ds(base + own, own), lanes] = im.astype(BF16)
-            hpart[f] += lax.dot_general(
-                eb[f, :, lanes],
+            hpart[f, some] += lax.dot_general(
+                eb[f, some, lanes],
                 src[f, :, lanes],
                 (((1,), (1,)), ((), ())),
                 preferred_element_type=F32,
             )
             return carry
 
-        hpart[f] = jnp.zeros(hpart.shape[1:], F32)
-        copies[f].wait()
+        hpart[f, some] = jnp.zeros(((hi - lo) * rows, heads2), F32)
+        if lo == 0:
+            prepare(f)
+            copies[f].wait()
         lax.fori_loop(0, panels // block, step, 0)
 
+    def loop_over(lo, hi, fn):
+        def step(o, carry):
+            fn(o)
+            return carry
+
+        lax.fori_loop(lo, hi, step, 0)
+
+    ring = npan // 2
+    side = pi // ring
+    away = ring * rows
+
+    def rs_size(f):
+        return ring if f else npan
+
     def rs_copy(f, o):
-        dest = (pi + o) % npan
+        dest = side * ring + (pi + o) % ring if f else (pi + o) % npan
         return pltpu.make_async_remote_copy(
             src_ref=hpart.at[f, pl.ds(pl.multiple_of(dest * rows, rows), rows)],
             dst_ref=rsbuf.at[f, o],
@@ -189,6 +210,23 @@
             device_id={"panel": dest},
             device_id_type=MESH,
         )
+
+    def pair_copy(f):
+        other = pl.multiple_of((1 - side) * away, away)
+        return pltpu.make_async_remote_copy(
+            src_ref=hpart.at[f, pl.ds(other, away)],
+            dst_ref=pairbuf.at[f],
+            send_sem=pair_send.at[f],
+            recv_sem=pair_recv.at[f],
+            device_id={"panel": (pi + ring) % npan},
+            device_id_type=MESH,
+        )
+
+    def spread(f):
+        pair_copy(f).wait_recv()
+        mine = pl.ds(pl.multiple_of(side * away, away), away)
+        hpart[f, mine] += pairbuf[f]
+        loop_over(1, ring, lambda o: rs_copy(f, o).start())
 
     def ag_copy(f, o):
         dest = (pi + o) % npan
@@ -212,17 +250,10 @@
             device_id_type=MESH,
         )
 
-    def loop_over(lo, hi, fn):
-        def step(o, carry):
-            fn(o)
-            return carry
-
-        lax.fori_loop(lo, hi, step, 0)
-
     def cotangent(f):
-        loop_over(1, npan, lambda o: rs_copy(f, o).wait_recv())
+        loop_over(1, rs_size(f), lambda o: rs_copy(f, o).wait_recv())
         total = hpart[f, pl.ds(pl.multiple_of(pi * rows, rows), rows), :]
-        for o in range(1, npan):
+        for o in range(1, rs_size(f)):
             total = total + rsbuf[f, o]
         top = total[:own]
         low = pltpu.roll(total[own:], heads, 1)
@@ -260,8 +291,8 @@
 
     sub = 256
 
-    def backward(f, xdest, side, dst):
-        j = xdest * 2 + side
+    def backward(f, xdest, column, dst):
+        j = xdest * 2 + column
 
         def step(n, carry):
             lanes = pl.ds(pl.multiple_of(j * block + n * sub, sub), sub)
@@ -293,9 +324,8 @@
             qc = k * jnp.sum(qc, axis=0, keepdims=True)
             qs = k * jnp.sum(qs, axis=0, keepdims=True)
             rs = jnp.sum(rs, axis=0, keepdims=True)
-            here = pl.ds(pl.multiple_of(n * sub, sub), sub)
             for r, value in enumerate((qc, qs, k * rs, rs)):
-                gsum[j, r : r + 1, here] += value
+                gsum[j, pl.ds(4 * n + r, 1), :] += value
             return carry
 
         lax.fori_loop(0, block // sub, step, 0)
@@ -375,18 +405,38 @@
         for c in x_copies(f, m):
             c.wait_recv()
 
+    def g_copy(b, o):
+        to = (di + o) % ndir
+        return pltpu.make_async_remote_copy(
+            src_ref=gsum.at[to],
+            dst_ref=gbuf.at[b, o],
+            send_sem=g_send.at[b, o],
+            recv_sem=g_recv.at[b, o],
+            device_id={"dir": to, "freq": (fi + b) % nfreq},
+            device_id_type=MESH,
+        )
+
+    def g_start(j, shifts):
+        o = (j - di + ndir) % ndir
+        for b in shifts:
+            g_copy(b, o).start()
+
     def to_sibling(f, n):
         backward(f, order[n], 1 - core, ssend.at[f, n])
         sib_copy(f, n).start()
+        if f == nf - 1:
+            g_start(order[n] * 2 + (1 - core), range(nfreq))
 
     def keep(f, n):
         backward(f, order[n], core, sown.at[f, n])
+        if f == nf - 1:
+            g_start(order[n] * 2 + core, range(1 if n == 3 else 0, nfreq))
 
     def join(f, n):
         sib_copy(f, n).wait_recv()
         sown[f, n] += sbuf[f, n]
 
-    def reverse(f):
+    def reverse(f, meanwhile=None):
         to_sibling(f, 0)
         keep(f, 0)
         to_sibling(f, 1)
@@ -401,6 +451,8 @@
         to_sibling(f, 3)
         join(f, 2)
         x_start(f, 4)
+        if meanwhile:
+            meanwhile()
         keep(f, 3)
 
     def relay(f):
@@ -419,31 +471,32 @@
         out_ref[f, upper] = total[:heads] + x_read(f, 3, 3) + x_read(f, 4, 3)
         out_ref[f, lower] = total[heads:] + x_read(f, 2, 3) + x_read(f, 5, 3)
 
-    def g_copy(b, o):
-        to = (di + o) % ndir
-        return pltpu.make_async_remote_copy(
-            src_ref=gsum.at[to],
-            dst_ref=gbuf.at[b, o],
-            send_sem=g_send.at[b, o],
-            recv_sem=g_recv.at[b, o],
-            device_id={"dir": to, "freq": (fi + b) % nfreq},
-            device_id_type=MESH,
-        )
-
-    for f in range(nf):
-        forward(f)
-        if f == 0:
-            pl.semaphore_wait(barrier, npan - 1 + nfreq * ndir - 1)
-        loop_over(1, npan, lambda o: rs_copy(f, o).start())
-    for f in range(nf):
-        cotangent(f)
+    def send_sums(f, lo, hi):
+        def one(dest):
+            o = (dest - pi + npan) % npan
+
+            @pl.when(o != 0)
+            def _():
+                rs_copy(f, o).start()
+
+        loop_over(lo, hi, one)
+
+    middle = npan // 2
+    forward(0, 0, middle)
+    pl.semaphore_wait(barrier, npan - 1 + nfreq * ndir - 1)
+    send_sums(0, 0, middle)
+    forward(0, middle, npan)
+    send_sums(0, middle, npan)
+    forward(1, 0, npan)
+    pair_copy(1).start()
+    cotangent(0)
+    spread(1)
+    cotangent(1)
     gather(0)
     reverse(0)
     gather(1)
     relay(0)
     reverse(1)
-    for b in range(nfreq):
-        loop_over(0 if b else 1, ndir, lambda o: g_copy(b, o).start())
     relay(1)
     finish(0)
     for b in range(nfreq):
@@ -452,13 +505,17 @@
     for b in range(nfreq):
         for o in range(0 if b else 1, ndir):
             total = total + gbuf[b, o]
-    area = geom_ref[3:4, pl.ds(pl.multiple_of(di * block, block), block)]
-    geo_ref[0:3, :] = shape_scale * total[0:3]
-    geo_ref[3:4, :] = shape_scale * (total[3:4] / area)
+    for n in range(block // sub):
+        here = pl.ds(n * sub, sub)
+        area = geom_ref[3:4, pl.ds(pl.multiple_of(di * block + n * sub, sub), sub)]
+        geo_ref[0:3, here] = shape_scale * total[4 * n : 4 * n + 3]
+        geo_ref[3:4, here] = shape_scale * (total[4 * n + 3 : 4 * n + 4] / area)
     finish(1)
 
     for f in range(nf):
-        loop_over(1, npan, lambda o: rs_copy(f, o).wait_send())
+        if f:
+            pair_copy(f).wait_send()
+        loop_over(1, rs_size(f), lambda o: rs_copy(f, o).wait_send())
         loop_over(1, npan, lambda o: ag_copy(f, o).wait_send())
         for n in range(4):
             sib_copy(f, n).wait_send()
@@ -467,6 +524,11 @@
                 c.wait_send()
     for b in range(nfreq):
         loop_over(0 if b else 1, ndir, lambda o: g_copy(b, o).wait_send())
+
+
+def hand_on(out_in, geo_in, out_ref, geo_ref):
+    out_ref[...] = out_in[...]
+    geo_ref[...] = geo_in[...]
 
 
 def direction_table():
@@ -509,6 +571,7 @@
                 vmem((nf, 2 * dirs, panels), F32),
                 vmem((nf, 2 * dirs, panels), BF16),
                 vmem((nf, 2 * dirs, heads2), F32),
+                vmem((nf, dirs, heads2), F32),
                 vmem((nf, npan, 2 * own, heads2), F32),
                 vmem((nf, npan, own, 2 * heads2), BF16),
                 vmem((nf, 2 * dirs, 2 * heads2), BF16),
@@ -521,8 +584,10 @@
                 vmem((nf, 6, heads, block), jnp.int16),
                 vmem((nf, 6, 8, 128), F32),
                 vmem((nf, 6, 8, 128), F32),
-                vmem((ndir, 8, block), F32),
-                vmem((nfreq, ndir, 8, block), F32),
+                vmem((ndir, 8, block // 2), F32),
+                vmem((nfreq, ndir, 8, block // 2), F32),
+                dma((nf,)),
+                dma((nf,)),
                 dma((nf,)),
                 dma((nf, npan)),
                 dma((nf, npan)),
@@ -546,6 +611,13 @@
             heading_dir.reshape(1, heads),
             jnp.asarray(direction_table()),
         )
+        out, geo = pl.pallas_call(
+            hand_on,
+            out_shape=(
+                jax.ShapeDtypeStruct(out.shape, F32),
+                jax.ShapeDtypeStruct(geo.shape, F32),
+            ),
+        )(out, geo)
         return out.reshape(nf, parts, heads, block), geo
 
     return jax.shard_map(

time: 60.3 us -> 56.2 us (0.932)
  local copies, waits for them, and re-layouts: 3.16 us -> 0 us
  Pallas kernels: 56.3 us -> 55.4 us
    unnamed x2 -> x0, local copies, waits for them, and re-layouts: 3.16 us -> none
    pallas_call x1, Pallas kernels: 56.3 us -> 53.5 us  [body(): pl.pallas_call(functools.partial(kernel, sizes), out_shape=(jax.ShapeDtyp...]
    pallas_call x0 -> x1, Pallas kernels: none -> 1.87 us  [body(): pl.pallas_call(hand_on, out_shape=(jax.ShapeDtypeStruct(out.shape, F32),...]
where the time goes in v3:
time: 56.2 us; the launch traced here: 56 us
  Pallas kernels  55.4 us (99%)
  between operations  0.64 us (1%)
    pallas_call x1, Pallas kernels, body(): pl.pallas_call(functools.partial(kernel, sizes), out_shape=(jax.ShapeDtyp...  53.5 us
    pallas_call x1, Pallas kernels, body(): pl.pallas_call(hand_on, out_shape=(jax.ShapeDtypeStruct(out.shape, F32),...  1.87 us

profile of v3, /device:TPU:1, one launch (start us, length us, event | category | flops | bytes accessed | tf_op | source)
XLA Modules:
  0.0 56.0 jit_solution(15789198078929684477)
XLA Ops:
  0.6 53.5 %shard_map.77 = (f32[2,128,512]{2,1,0:T(8,128)}, f32[4,512]{1,0:T(4,128)}) custom-call(bf16[2,128,4096]{2,1,0:T(8,128)(2,1)} %bitcast.3, f32[4,4096]{1,0:T(4,128)} %geom_ref.1, f32[2,64]{1,0:T(2,128)} %cot_ref.1, s32[2]{0:T(128)} %fidx_ref.1, s32[1,64]{1,0:T(1,128)} %bitcast.4, f32[2,16,128]{2,1,0:T(8,128)} %constant.2.clone.table_ref), custom_call_target="tpu_custom_call" | custom-call | tf_op jit(solution)/shard_map/pallas_call | solution.py:551
  54.1 1.9 %shard_map.78 = (f32[2,128,512]{2,1,0:T(8,128)}, f32[4,512]{1,0:T(4,128)}) custom-call(f32[2,128,512]{2,1,0:T(8,128)} %get-tuple-element.6.out_in, f32[4,512]{1,0:T(4,128)} %get-tuple-element.7.geo_in), custom_call_target="tpu_custom_call" | custom-call | tf_op jit(solution)/shard_map/pallas_call | solution.py:614

commit v4 on v3

--- a/solution.py
+++ b/solution.py
@@ -34,7 +34,7 @@
 
 
 SIN_COEF = fit_even(lambda t: np.sinc(np.sqrt(t)) * np.pi, 3)
-COS_COEF = fit_even(lambda t: np.cos(np.pi * np.sqrt(t)), 4)
+COS_COEF = fit_even(lambda t: np.cos(np.pi * np.sqrt(t)), 3)
 
 
 def horner(coef, t):
@@ -196,6 +196,7 @@
     ring = npan // 2
     side = pi // ring
     away = ring * rows
+    far_first = sorted(range(ring), key=lambda o: -min(o, ring - o))
 
     def rs_size(f):
         return ring if f else npan
@@ -226,7 +227,8 @@
         pair_copy(f).wait_recv()
         mine = pl.ds(pl.multiple_of(side * away, away), away)
         hpart[f, mine] += pairbuf[f]
-        loop_over(1, ring, lambda o: rs_copy(f, o).start())
+        for o in far_first[:-1]:
+            rs_copy(f, o).start()
 
     def ag_copy(f, o):
         dest = (pi + o) % npan
@@ -273,7 +275,10 @@
         near = weight * (along * (top - low) - hit)
         far = weight * (-along * (top + low) - hit_far)
         gall[f, pi] = jnp.concatenate([near, far], axis=1).astype(BF16)
-        loop_over(1, npan, lambda o: ag_copy(f, o).start())
+        for near in far_first:
+            for o in (near, near + ring):
+                if o:
+                    ag_copy(f, o).start()
 
     def gather(f):
         loop_over(1, npan, lambda o: ag_arrival(f, o).wait_recv())
@@ -471,22 +476,21 @@
         out_ref[f, upper] = total[:heads] + x_read(f, 3, 3) + x_read(f, 4, 3)
         out_ref[f, lower] = total[heads:] + x_read(f, 2, 3) + x_read(f, 5, 3)
 
-    def send_sums(f, lo, hi):
-        def one(dest):
+    def send_sums(half):
+        for near in far_first:
+            dest = half * ring + (pi + near) % ring
             o = (dest - pi + npan) % npan
 
             @pl.when(o != 0)
             def _():
-                rs_copy(f, o).start()
-
-        loop_over(lo, hi, one)
+                rs_copy(0, o).start()
 
     middle = npan // 2
     forward(0, 0, middle)
     pl.semaphore_wait(barrier, npan - 1 + nfreq * ndir - 1)
-    send_sums(0, 0, middle)
+    send_sums(0)
     forward(0, middle, npan)
-    send_sums(0, middle, npan)
+    send_sums(1)
     forward(1, 0, npan)
     pair_copy(1).start()
     cotangent(0)
@@ -494,10 +498,9 @@
     cotangent(1)
     gather(0)
     reverse(0)
+    relay(0)
     gather(1)
-    relay(0)
-    reverse(1)
-    relay(1)
+    reverse(1, lambda: relay(1))
     finish(0)
     for b in range(nfreq):
         loop_over(0 if b else 1, ndir, lambda o: g_copy(b, o).wait_recv())

time: 56.2 us -> 54.7 us (0.973)
  Pallas kernels: 55.4 us -> 53.9 us
    pallas_call x1, Pallas kernels: 53.5 us -> 52 us  [body(): pl.pallas_call(functools.partial(kernel, sizes), out_shape=(jax.ShapeDtyp...]
where the time goes in v4:
time: 54.7 us; the launch traced here: 54.5 us
  Pallas kernels  53.9 us (99%)
  between operations  0.64 us (1%)
    pallas_call x1, Pallas kernels, body(): pl.pallas_call(functools.partial(kernel, sizes), out_shape=(jax.ShapeDtyp...  52 us
    pallas_call x1, Pallas kernels, body(): pl.pallas_call(hand_on, out_shape=(jax.ShapeDtypeStruct(out.shape, F32),...  1.87 us

profile of v4, /device:TPU:1, one launch (start us, length us, event | category | flops | bytes accessed | tf_op | source)
XLA Modules:
  0.0 54.5 jit_solution(10292922158565635519)
XLA Ops:
  0.6 52.0 %shard_map.77 = (f32[2,128,512]{2,1,0:T(8,128)}, f32[4,512]{1,0:T(4,128)}) custom-call(bf16[2,128,4096]{2,1,0:T(8,128)(2,1)} %bitcast.3, f32[4,4096]{1,0:T(4,128)} %geom_ref.1, f32[2,64]{1,0:T(2,128)} %cot_ref.1, s32[2]{0:T(128)} %fidx_ref.1, s32[1,64]{1,0:T(1,128)} %bitcast.4, f32[2,16,128]{2,1,0:T(8,128)} %constant.2.clone.table_ref), custom_call_target="tpu_custom_call" | custom-call | tf_op jit(solution)/shard_map/pallas_call | solution.py:554
  52.7 1.9 %shard_map.78 = (f32[2,128,512]{2,1,0:T(8,128)}, f32[4,512]{1,0:T(4,128)}) custom-call(f32[2,128,512]{2,1,0:T(8,128)} %get-tuple-element.6.out_in, f32[4,512]{1,0:T(4,128)} %get-tuple-element.7.geo_in), custom_call_target="tpu_custom_call" | custom-call | tf_op jit(solution)/shard_map/pallas_call | solution.py:617

commit v5 on v4

--- a/solution.py
+++ b/solution.py
@@ -152,14 +152,14 @@
         vecs[f, 4:5, :] = k
         vecs[f, 5:6, :] = 1.0 / amp
 
-    def forward(f, lo, hi):
-        some = pl.ds(lo * rows, (hi - lo) * rows)
+    def forward(f, lo, count, first):
+        some = pl.ds(pl.multiple_of(lo * rows, count * rows), count * rows)
 
         def step(b, carry):
             lanes = pl.ds(pl.multiple_of(b * block, block), block)
 
-            for g in range(lo, hi):
-                at = pl.ds(g * own, own)
+            for g in range(count):
+                at = pl.ds(pl.multiple_of((lo + g) * own, own), own)
                 ct = jnp.concatenate([ctab[at, :]] * (block // 128), axis=1)
                 st = jnp.concatenate([stab[at, :]] * (block // 128), axis=1)
                 turns = vecs[f, 0:1, lanes] * ct + vecs[f, 1:2, lanes] * st
@@ -167,7 +167,7 @@
                 q = s * vecs[f, 3:4, lanes]
                 re = vecs[f, 2:3, lanes] + q * s
                 im = q * c
-                base = g * rows
+                base = pl.multiple_of((lo + g) * rows, rows)
                 ef[f, pl.ds(base, own), lanes] = re
                 ef[f, pl.ds(base + own, own), lanes] = im
                 eb[f, pl.ds(base, own), lanes] = re.astype(BF16)
@@ -180,8 +180,8 @@
             )
             return carry
 
-        hpart[f, some] = jnp.zeros(((hi - lo) * rows, heads2), F32)
-        if lo == 0:
+        hpart[f, some] = jnp.zeros((count * rows, heads2), F32)
+        if first:
             prepare(f)
             copies[f].wait()
         lax.fori_loop(0, panels // block, step, 0)
@@ -486,13 +486,14 @@
                 rs_copy(0, o).start()
 
     middle = npan // 2
-    forward(0, 0, middle)
+    forward(0, 0, middle, True)
     pl.semaphore_wait(barrier, npan - 1 + nfreq * ndir - 1)
     send_sums(0)
-    forward(0, middle, npan)
+    forward(0, middle, middle, False)
     send_sums(1)
-    forward(1, 0, npan)
+    forward(1, (1 - side) * middle, middle, True)
     pair_copy(1).start()
+    forward(1, side * middle, middle, False)
     cotangent(0)
     spread(1)
     cotangent(1)

time: 54.7 us -> 53.4 us (0.976)
  Pallas kernels: 53.9 us -> 52.6 us
    pallas_call x1, Pallas kernels: 52 us -> 50.7 us  [body(): pl.pallas_call(functools.partial(kernel, sizes), out_shape=(jax.ShapeDtyp...]
where the time goes in v5:
time: 53.4 us; the launch traced here: 53.2 us
  Pallas kernels  52.6 us (99%)
  between operations  0.64 us (1%)
    pallas_call x1, Pallas kernels, body(): pl.pallas_call(functools.partial(kernel, sizes), out_shape=(jax.ShapeDtyp...  50.7 us
    pallas_call x1, Pallas kernels, body(): pl.pallas_call(hand_on, out_shape=(jax.ShapeDtypeStruct(out.shape, F32),...  1.87 us

profile of v5, /device:TPU:1, one launch (start us, length us, event | category | flops | bytes accessed | tf_op | source)
XLA Modules:
  0.0 53.2 jit_solution(12902412853456273016)
XLA Ops:
  0.6 50.7 %shard_map.77 = (f32[2,128,512]{2,1,0:T(8,128)}, f32[4,512]{1,0:T(4,128)}) custom-call(bf16[2,128,4096]{2,1,0:T(8,128)(2,1)} %bitcast.3, f32[4,4096]{1,0:T(4,128)} %geom_ref.1, f32[2,64]{1,0:T(2,128)} %cot_ref.1, s32[2]{0:T(128)} %fidx_ref.1, s32[1,64]{1,0:T(1,128)} %bitcast.4, f32[2,16,128]{2,1,0:T(8,128)} %constant.2.clone.table_ref), custom_call_target="tpu_custom_call" | custom-call | tf_op jit(solution)/shard_map/pallas_call | solution.py:555
  51.3 1.9 %shard_map.78 = (f32[2,128,512]{2,1,0:T(8,128)}, f32[4,512]{1,0:T(4,128)}) custom-call(f32[2,128,512]{2,1,0:T(8,128)} %get-tuple-element.6.out_in, f32[4,512]{1,0:T(4,128)} %get-tuple-element.7.geo_in), custom_call_target="tpu_custom_call" | custom-call | tf_op jit(solution)/shard_map/pallas_call | solution.py:618
